TPU v7x, 32 devices: a whole 2x2x4 slice. The times are simulated.
32 devices in a mesh: cells: 2 (over y), genes: 16 (over z, x, core).
Axes of the slice: x: 2, y: 2, z: 4, core: 2. Of those that a mesh axis runs over, the one named last changes fastest.
Arguments:
- expression: float32 [320, 32768], P('cells', 'genes'), may hold values from -6 to 6
- omega_diag: float32 [128, 256, 256], P('genes'), may hold values from -0.25 to 2, as said below
- omega_offd: float32 [128, 6, 256, 256], P('genes'), may hold values from -0.3 to 0.3
- omega_src: int32 [128, 6], replicated, may hold values from 0 to 15, all different within a row; in each aligned block of 8 rows (0 to 7, 8 to 15, ...) at most 3 rows name the same one
- omega_off: int32 [128, 6], replicated, may hold values from 0 to 6
Outputs:
- new_diag: float32 [128, 256, 256], P(('genes', 'cells'))
- new_offd: float32 [128, 6, 256, 256], P(('genes', 'cells'))
Inputs may be any that keep to these rules, and one draw needn't show every extreme that they name: `omega_src`: the 6 values of one row are distinct. Among the 8 rows of one index of genes (rows i * 8 to (i+1) * 8 - 1) no value appears more than 3 times, and in every draw some such group of rows names some value exactly 3 times. `omega_diag`: diagonal entries lie in 0.5 to 2; all other entries lie in -0.25 to 0.25.
All inputs are finite; a program needn't handle non-finite values.
Results may differ from a plain program's by a relative error of at most 0.000075.
Values sent between devices are 32-bit elements; how exact they have to be, the bound alone decides.
A program may use at most 192 MiB of HBM per device.

v0:
```python
import jax
import jax.numpy as jnp
from jax import lax
from jax.sharding import PartitionSpec as P


def stored_rows(omega_src, omega_off, per_dev):
    cols = lax.broadcasted_iota(jnp.int32, omega_src.shape, 0)
    bump = jnp.logical_and(omega_src == cols // per_dev, omega_off >= cols % per_dev).astype(
        jnp.int32
    )
    return omega_src * per_dev + omega_off + bump


def slot_ranks(src_groups, count):
    onehot = (src_groups[:, :, None] == lax.broadcasted_iota(jnp.int32, (1, 1, count), 2)).astype(
        jnp.int32
    )
    ranks = jnp.cumsum(onehot, axis=1) - 1
    return jnp.sum(onehot * ranks, axis=2)


def shrink(values, limit):
    return values - jnp.clip(values, -limit, limit)


def partials(own_x, own_y, far_x, far_y):
    highest = lax.Precision.HIGHEST
    diag_part = jnp.einsum("cjb,cje->jbe", own_x, own_y, precision=highest)
    diag_part = diag_part + jnp.swapaxes(diag_part, 1, 2)
    off_part = jnp.einsum("cjkb,cje->jkbe", far_x, own_y, precision=highest)
    off_part = off_part + jnp.einsum("cjkb,cje->jkbe", far_y, own_x, precision=highest)
    return (diag_part, off_part)


def per_device(expression, omega_diag, omega_offd, omega_src, omega_off):
    highest = lax.Precision.HIGHEST
    groups = lax.axis_size("genes")
    here = lax.axis_index("genes")
    per_dev = omega_diag.shape[0]
    fan = omega_src.shape[1]
    width = omega_diag.shape[1]
    cell_rows = expression.shape[0]
    most = max(2, (per_dev * fan + groups - 1) // groups)
    rows = stored_rows(omega_src, omega_off, per_dev)
    src_groups = omega_src.reshape(groups, per_dev * fan)
    local_groups = (rows % per_dev).reshape(groups, per_dev * fan)
    slots = slot_ranks(src_groups, groups)
    slot_iota = lax.broadcasted_iota(jnp.int32, (1, 1, most), 2)
    match = jnp.logical_and(
        (src_groups == here)[:, :, None], slots[:, :, None] == slot_iota
    ).astype(jnp.int32)
    send_index = jnp.sum(match * local_groups[:, :, None], axis=1).reshape(-1)
    mine_src = lax.dynamic_index_in_dim(src_groups, here, 0, keepdims=False)
    mine_slot = lax.dynamic_index_in_dim(slots, here, 0, keepdims=False)
    pick = mine_src * most + mine_slot
    local_x = expression.reshape(cell_rows, per_dev, width)
    sent_x = jnp.take(local_x, send_index, axis=1).reshape(cell_rows, groups, most, width)
    came_x = lax.all_to_all(sent_x, "genes", split_axis=1, concat_axis=1, tiled=True)
    far_x = jnp.take(came_x.reshape(cell_rows, groups * most, width), pick, axis=1).reshape(
        cell_rows, per_dev, fan, width
    )
    own_y = jnp.einsum("cjb,jbe->cje", local_x, omega_diag, precision=highest)
    own_y = own_y + jnp.einsum("cjkb,jkbe->cje", far_x, omega_offd, precision=highest)
    sent_y = jnp.take(own_y, send_index, axis=1).reshape(cell_rows, groups, most, width)
    came_y = lax.all_to_all(sent_y, "genes", split_axis=1, concat_axis=1, tiled=True)
    far_y = jnp.take(came_y.reshape(cell_rows, groups * most, width), pick, axis=1).reshape(
        cell_rows, per_dev, fan, width
    )
    share = per_dev // lax.axis_size("cells")
    where = lax.axis_index("cells")
    diag_part, off_part = partials(local_x, own_y, far_x, far_y)
    diag_sum, off_sum = (
        lax.psum_scatter(diag_part, "cells", scatter_dimension=0, tiled=True),
        lax.psum_scatter(off_part, "cells", scatter_dimension=0, tiled=True),
    )
    mine_diag = lax.dynamic_slice_in_dim(omega_diag, where * share, share, 0)
    mine_off = lax.dynamic_slice_in_dim(omega_offd, where * share, share, 0)
    step_size = 0.5
    limit = step_size * 0.04
    scale = 1.0 / (2.0 * cell_rows * lax.axis_size("cells"))
    eye = (
        lax.broadcasted_iota(jnp.int32, (width, width), 0)
        == lax.broadcasted_iota(jnp.int32, (width, width), 1)
    ).astype(jnp.float32)
    entries = jnp.sum(mine_diag * eye, axis=2)
    grad_diag = diag_sum * scale - eye * (1.0 / entries)[:, :, None]
    moved = mine_diag - step_size * grad_diag
    new_diag = eye * moved + (1.0 - eye) * shrink(moved, limit)
    new_offd = shrink(mine_off - step_size * (off_sum * scale), limit)
    return (new_diag, new_offd)


def solution(mesh):
    return jax.shard_map(
        per_device,
        mesh=mesh,
        in_specs=(
            P("cells", "genes"),
            P("genes", None, None),
            P("genes", None, None, None),
            P(),
            P(),
        ),
        out_specs=(P(("genes", "cells"), None, None), P(("genes", "cells"), None, None, None)),
        check_vma=False,
    )
```

profile of v0, /device:TPU:0, one launch (start us, length us, event | category | flops | bytes accessed | tf_op | source)
XLA Modules:
  0.0 617.5 jit_solution(4547552836912149609)
XLA Ops:
  12.1 4.2 gather_fusion
  16.3 7.9 %broadcast_select_fusion.3 = f32[48,160,256]{2,1,0:T(8,128)} fusion(f32[48,160,256]{2,1,0:T(8,128)} %gather_fusion, pred[48]{0:T(512)(128)(4,1)S(1)} %compare_and_fusion.1), kind=kLoop, calls=%fused_computation.9 | loop fusion | flops 1966080 | bytes 15728688 | tf_op jit(solution)/shard_map/jit(_take)/select_n | solution.py:58
  24.2 7.4 %all-to-all-start = ((f32[160,16,3,256]{3,0,2,1:T(8,128)}), f32[160,16,3,256]{3,0,2,1:T(8,128)}, u32[]{:S(2)}, u32[]{:S(2)}) async-start(f32[160,16,3,256]{3,0,2,1:T(8,128)} %bitcast.50), calls=%async_computation | async-start | bytes 15728640 | tf_op jit(solution)/shard_map/all_to_all | solution.py:59
  31.8 141.2 %all-to-all-done = f32[160,16,3,256]{3,0,2,1:T(8,128)} async-done(((f32[160,16,3,256]{3,0,2,1:T(8,128)}), f32[160,16,3,256]{3,0,2,1:T(8,128)}, u32[]{:S(2)}, u32[]{:S(2)}) %all-to-all-start) | async-done | bytes 7864352 | tf_op jit(solution)/shard_map/all_to_all | solution.py:59
  173.1 7.4 %gather_fusion.1 = f32[48,160,256]{2,1,0:T(8,128)} fusion(f32[160,48,256]{2,0,1:T(8,128)} %bitcast.3, s32[1024]{0:T(1024)S(1)} %pad_clamp_fusion), kind=kCustom, calls=%fused_computation.1.clone | custom fusion | bytes 15728832 | tf_op jit(solution)/shard_map/jit(_take)/gather | solution.py:60
  180.5 4.7 broadcast_select_fusion.2
  185.2 14.2 %convolution_bitcast_fusion.1 = f32[160,8,256]{2,0,1:T(8,128)S(1)} fusion(f32[160,8,6,256]{3,0,2,1:T(8,128)S(1)} %bitcast.46, f32[8,6,256,256]{3,2,1,0:T(8,128)} %param.11), kind=kOutput, calls=%fused_computation.14 | convolution fusion | flops 6039797760 | bytes 21757952 | tf_op jit(solution)/shard_map/cjkb,jkbe->cje/dot_general | solution.py:64
  199.5 3.2 fusion
  202.7 4.2 gather_fusion.2
  206.8 7.8 %broadcast_select_fusion.1 = f32[48,160,256]{2,1,0:T(8,128)} fusion(f32[48,160,256]{2,1,0:T(8,128)} %gather_fusion.2, pred[48]{0:T(512)(128)(4,1)S(1)} %compare_and_fusion.1), kind=kLoop, calls=%fused_computation.7 | loop fusion | flops 1966080 | bytes 15728688 | tf_op jit(solution)/shard_map/jit(_take)/select_n | solution.py:65
  214.6 34.4 %all-to-all-start.1 = ((f32[160,16,3,256]{3,0,2,1:T(8,128)}), f32[160,16,3,256]{3,0,2,1:T(8,128)}, u32[]{:S(2)}, u32[]{:S(2)}) async-start(f32[160,16,3,256]{3,0,2,1:T(8,128)} %bitcast.49), calls=%async_computation.2 | async-start | bytes 15728640 | tf_op jit(solution)/shard_map/all_to_all | solution.py:66
  249.4 4.8 fusion.13
  254.2 2.9 copy.53
  257.1 3.8 bitcast_add_fusion
  261.0 1.5 copy.61
  262.5 24.7 %fusion.1 = f32[8,6,256,256]{3,2,1,0:T(8,128)} fusion(f32[160,8,6,256]{3,0,2,1:T(8,128)} %bitcast.47, f32[160,8,256]{2,0,1:T(8,128)S(1)} %fusion), kind=kOutput, calls=%fused_computation.16 | convolution fusion | flops 6039797760 | bytes 21757952 | tf_op jit(solution)/shard_map/cjkb,cje->jkbe/dot_general | solution.py:31
  287.2 103.3 %all-to-all-done.1 = f32[160,16,3,256]{3,0,2,1:T(8,128)} async-done(((f32[160,16,3,256]{3,0,2,1:T(8,128)}), f32[160,16,3,256]{3,0,2,1:T(8,128)}, u32[]{:S(2)}, u32[]{:S(2)}) %all-to-all-start.1) | async-done | bytes 7864352 | tf_op jit(solution)/shard_map/all_to_all | solution.py:66
  390.5 7.4 %gather_fusion.3 = f32[48,160,256]{2,1,0:T(8,128)} fusion(f32[160,48,256]{2,0,1:T(8,128)} %bitcast.15, s32[1024]{0:T(1024)S(1)} %pad_clamp_fusion), kind=kCustom, calls=%fused_computation.3.clone | custom fusion | bytes 15728832 | tf_op jit(solution)/shard_map/jit(_take)/gather | solution.py:67
  397.9 4.2 broadcast_select_fusion
  402.1 25.1 %convolution_add_fusion = f32[8,6,256,256]{3,2,1,0:T(8,128)} fusion(f32[8,6,256,256]{3,2,1,0:T(8,128)} %fusion.1, f32[160,8,6,256]{3,0,2,1:T(8,128)S(1)} %bitcast.51, f32[160,8,256,1]{2,1,0,3:T(8,128)S(1)} %bitcast.56), kind=kOutput, calls=%fused_computation.5 | convolution fusion | flops 6042943488 | bytes 34340864 | tf_op jit(solution)/shard_map/cjkb,cje->jkbe/dot_general | solution.py:32
  427.3 1.5 copy-done.2
  429.1 2.6 fusion.5
  431.7 170.1 %reduce-scatter.5.cloned.1.call-done = f32[4,6,256,256]{3,2,1,0:T(8,128)} async-done(((f32[8,6,256,256]{3,2,1,0:T(8,128)}), f32[4,6,256,256]{3,2,1,0:T(8,128)}) %reduce-scatter.5.cloned.1.call-update) | async-done | bytes 6291472 | tf_op jit(solution)/shard_map/reduce_scatter | solution.py:75
  601.8 8.9 %clamp_subtract_fusion = f32[4,6,256,256]{3,2,1,0:T(8,128)} fusion(f32[4,6,256,256]{3,2,1,0:T(8,128)} %reduce-scatter.5.cloned.1.call-done, f32[8,6,256,256]{3,2,1,0:T(8,128)} %param.11, s32[]{:T(128)S(6)} %select_n.38), kind=kLoop, calls=%fused_computation.4 | loop fusion | flops 6291456 | bytes 18874372 | tf_op jit(solution)/shard_map/sub | solution.py:24
  (39 shorter events, 5.7 us)
Async XLA Ops:
  24.2 148.9 %all-to-all-start = ((f32[160,16,3,256]{3,0,2,1:T(8,128)}), f32[160,16,3,256]{3,0,2,1:T(8,128)}, u32[]{:S(2)}, u32[]{:S(2)}) async-start(f32[160,16,3,256]{3,0,2,1:T(8,128)} %bitcast.50), calls=%async_computation | async-start | bytes 15728640 | tf_op jit(solution)/shard_map/all_to_all | solution.py:59
  185.2 14.2 %copy-start = (f32[48,160,256]{2,1,0:T(8,128)}, f32[48,160,256]{2,1,0:T(8,128)S(1)}, u32[]{:S(2)}) copy-start(f32[48,160,256]{2,1,0:T(8,128)S(1)} %broadcast_select_fusion.2) | copy-start | bytes 23592964
  185.2 14.2 %copy-start.1 = (f32[160,2048]{1,0:T(8,128)S(1)}, f32[160,2048]{1,0:T(8,128)}, u32[]{:S(2)}) copy-start(f32[160,2048]{1,0:T(8,128)} %param.9) | copy-start | bytes 3932164
  214.6 175.9 %all-to-all-start.1 = ((f32[160,16,3,256]{3,0,2,1:T(8,128)}), f32[160,16,3,256]{3,0,2,1:T(8,128)}, u32[]{:S(2)}, u32[]{:S(2)}) async-start(f32[160,16,3,256]{3,0,2,1:T(8,128)} %bitcast.49), calls=%async_computation.2 | async-start | bytes 15728640 | tf_op jit(solution)/shard_map/all_to_all | solution.py:66
  249.1 180.0 %reduce-scatter.3.cloned.1.call-start = ((), (), s32[]{:S(2)}) async-start(), calls=%async_computation.4 | async-start | bytes 3145728 | tf_op jit(solution)/shard_map/reduce_scatter | solution.py:74
  261.0 340.8 %reduce-scatter.5.cloned.1.call-start = ((), (), s32[]{:S(2)}) async-start(), calls=%async_computation.5 | async-start | bytes 18874368 | tf_op jit(solution)/shard_map/reduce_scatter | solution.py:75
  397.9 4.2 copy-start.3
  427.2 1.6 copy-start.2
Sparse Core Ops, SparseCore 0:
  261.1 33.2 reduce-scatter.2
  427.4 174.3 reduce-scatter.4
where the time goes:
time: 618 us; the launch traced here: 617 us
  waiting for transfers between devices  415 us (67%)
  matrix products  72 us (12%)
  other arithmetic  42.4 us (7%)
  starting transfers between devices  42.2 us (7%)
  local copies, waits for them, and re-layouts  32 us (5%)
  between operations  14.3 us (2%)
    reduce_scatter x1, waiting for transfers between devices, per_device(): lax.psum_scatter(off_part, 'cells', scatter_dimension=0, tiled=True)  170 us
    all_to_all x1, waiting for transfers between devices, per_device(): lax.all_to_all(sent_x, 'genes', split_axis=1, concat_axis=1, tiled=True)  141 us
    all_to_all x1, waiting for transfers between devices, per_device(): lax.all_to_all(sent_y, 'genes', split_axis=1, concat_axis=1, tiled=True)  103 us
    all_to_all x1, starting transfers between devices, per_device(): lax.all_to_all(sent_y, 'genes', split_axis=1, concat_axis=1, tiled=True)  34.4 us
    dot_general x1, matrix products, partials(): jnp.einsum('cjkb,cje->jkbe', far_y, own_x, precision=highest)  25.1 us
    dot_general x1, matrix products, partials(): off_part = jnp.einsum('cjkb,cje->jkbe', far_x, own_y, precision=highest)  24.7 us
    dot_general x1, matrix products, per_device(): jnp.einsum('cjkb,jkbe->cje', far_x, omega_offd, precision=highest)  14.2 us
  transfers between devices with their start and end apart: 4, of which 3 were waited for; matrix products, arithmetic and copies ran while one was open for 13% of the time, Pallas kernels for 0%

commit v1 on v0

v1 whole, which is shorter than its diff:
```python
import jax
import jax.numpy as jnp
from jax import lax
from jax.sharding import PartitionSpec as P


def stored_rows(omega_src, omega_off, per_dev):
    cols = lax.broadcasted_iota(jnp.int32, omega_src.shape, 0)
    bump = jnp.logical_and(omega_src == cols // per_dev, omega_off >= cols % per_dev).astype(
        jnp.int32
    )
    return omega_src * per_dev + omega_off + bump


def shrink(values, limit):
    return values - jnp.clip(values, -limit, limit)


def exchange(shard, table):
    whole = lax.all_gather(shard, "genes", axis=0, tiled=True)
    picked = jnp.take(whole, table, axis=0)
    return lax.all_to_all(picked, "cells", split_axis=0, concat_axis=1, tiled=True)


def per_device(expression, omega_diag, omega_offd, omega_src, omega_off):
    high = lax.Precision.HIGH
    here = lax.axis_index("genes")
    where = lax.axis_index("cells")
    cells = lax.axis_size("cells")
    per_dev, width = omega_diag.shape[:2]
    fan = omega_src.shape[1]
    cell_rows = expression.shape[0]
    share = per_dev // cells
    all_rows = cells * cell_rows
    rows = stored_rows(omega_src, omega_off, per_dev)
    table = lax.dynamic_slice_in_dim(rows, here * per_dev, per_dev, 0).reshape(-1)
    mine_diag = lax.dynamic_slice_in_dim(omega_diag, where * share, share, 0)
    mine_off = lax.dynamic_slice_in_dim(omega_offd, where * share, share, 0)

    shard_x = jnp.swapaxes(expression.reshape(cell_rows, per_dev, width), 0, 1)
    own_x = lax.all_to_all(shard_x, "cells", split_axis=0, concat_axis=1, tiled=True)
    far_x = exchange(shard_x, table).reshape(share, fan, all_rows, width)
    own_y = jnp.einsum("jcb,jbe->jce", own_x, mine_diag, precision=high)
    own_y = own_y + jnp.einsum("jkcb,jkbe->jce", far_x, mine_off, precision=high)
    shard_y = lax.all_to_all(own_y, "cells", split_axis=1, concat_axis=0, tiled=True)
    far_y = exchange(shard_y, table).reshape(share, fan, all_rows, width)
    diag_sum = jnp.einsum("jcb,jce->jbe", own_x, own_y, precision=high)
    diag_sum = diag_sum + jnp.swapaxes(diag_sum, 1, 2)
    off_sum = jnp.einsum("jkcb,jce->jkbe", far_x, own_y, precision=high)
    off_sum = off_sum + jnp.einsum("jkcb,jce->jkbe", far_y, own_x, precision=high)

    step_size = 0.5
    limit = step_size * 0.04
    scale = 1.0 / (2.0 * all_rows)
    eye = (
        lax.broadcasted_iota(jnp.int32, (width, width), 0)
        == lax.broadcasted_iota(jnp.int32, (width, width), 1)
    ).astype(jnp.float32)
    entries = jnp.sum(mine_diag * eye, axis=2)
    grad_diag = diag_sum * scale - eye * (1.0 / entries)[:, :, None]
    moved = mine_diag - step_size * grad_diag
    new_diag = eye * moved + (1.0 - eye) * shrink(moved, limit)
    new_offd = shrink(mine_off - step_size * (off_sum * scale), limit)
    return (new_diag, new_offd)


def solution(mesh):
    return jax.shard_map(
        per_device,
        mesh=mesh,
        in_specs=(
            P("cells", "genes"),
            P("genes", None, None),
            P("genes", None, None, None),
            P(),
            P(),
        ),
        out_specs=(P(("genes", "cells"), None, None), P(("genes", "cells"), None, None, None)),
        check_vma=False,
    )
```

time: 618 us -> 516 us (0.83)
  waiting for transfers between devices: 415 us -> 368 us
  matrix products: 72 us -> 35.9 us
  starting transfers between devices: 42.2 us -> 18.1 us
  other arithmetic: 42.4 us -> 20.4 us
  blocking collectives: 0 us -> 18.7 us
  local copies, waits for them, and re-layouts: 32 us -> 39.8 us
    all_gather x0 -> x2, waiting for transfers between devices: none -> 215 us  [exchange(): whole = lax.all_gather(shard, 'genes', axis=0, tiled=True)]
    reduce_scatter x2 -> x0, waiting for transfers between devices: 170 us -> none  [the longest x1 170 us: per_device(): lax.psum_scatter(off_part, 'cells', scatter_dimension=0, tiled=True)]
    all_to_all x2 -> x3, waiting for transfers between devices: 245 us -> 153 us  [the longest x2 153 us: exchange(): lax.all_to_all(picked, 'cells', split_axis=0, concat_axis=1, tiled=True)]
    dot_general x5, matrix products: 72 us -> 35.9 us  [the longest x1 12.7 us: per_device(): jnp.einsum('jkcb,jce->jkbe', far_y, own_x, precision=high)]
    all_to_all x2 -> x3, starting transfers between devices: 41.9 us -> 18 us  [the longest x2 13.7 us: exchange(): lax.all_to_all(picked, 'cells', split_axis=0, concat_axis=1, tiled=True)]
    all_to_all x0 -> x1, blocking collectives: none -> 18.7 us  [per_device(): lax.all_to_all(own_y, 'cells', split_axis=1, concat_axis=0, tiled=True)]
    select_n x7 -> x3, other arithmetic: 25.3 us -> 15.6 us  [exchange(): picked = jnp.take(whole, table, axis=0)]
    all_to_all x0 -> x5, local copies, waits for them, and re-layouts: none -> 9.59 us  [the longest x2 8.05 us: exchange(): lax.all_to_all(picked, 'cells', split_axis=0, concat_axis=1, tiled=True)]
  transfers between devices with their start and end apart: 4 -> 5, of which waited for: 3 -> 4; matrix products, arithmetic and copies ran while one was open for 13% -> 8% of each run, Pallas kernels for 0% -> 0%
where the time goes in v1:
time: 516 us; the launch traced here: 515 us
  waiting for transfers between devices  368 us (71%)
  local copies, waits for them, and re-layouts  39.8 us (8%)
  matrix products  35.9 us (7%)
  other arithmetic  20.4 us (4%)
  blocking collectives  18.7 us (4%)
  starting transfers between devices  18.1 us (4%)
  between operations  14.2 us (3%)
    all_gather x2, waiting for transfers between devices, exchange(): whole = lax.all_gather(shard, 'genes', axis=0, tiled=True)  215 us
    all_to_all x2, waiting for transfers between devices, exchange(): lax.all_to_all(picked, 'cells', split_axis=0, concat_axis=1, tiled=True)  153 us
    gather x2, local copies, waits for them, and re-layouts, exchange(): picked = jnp.take(whole, table, axis=0)  22.2 us
    all_to_all x1, blocking collectives, per_device(): lax.all_to_all(own_y, 'cells', split_axis=1, concat_axis=0, tiled=True)  18.7 us
    select_n x3, other arithmetic, exchange(): picked = jnp.take(whole, table, axis=0)  15.6 us
    all_to_all x2, starting transfers between devices, exchange(): lax.all_to_all(picked, 'cells', split_axis=0, concat_axis=1, tiled=True)  13.7 us
    dot_general x1, matrix products, per_device(): jnp.einsum('jkcb,jce->jkbe', far_y, own_x, precision=high)  12.7 us
    dot_general x1, matrix products, per_device(): off_sum = jnp.einsum('jkcb,jce->jkbe', far_x, own_y, precision=high)  11.5 us
  transfers between devices with their start and end apart: 5, of which 4 were waited for; matrix products, arithmetic and copies ran while one was open for 8% of the time, Pallas kernels for 0%

profile of v1, /device:TPU:0, one launch (start us, length us, event | category | flops | bytes accessed | tf_op | source)
XLA Modules:
  0.0 515.4 jit_solution(14371886521751001108)
XLA Ops:
  7.2 1.8 copy.53
  9.0 1.5 copy.40
  10.5 4.3 all-to-all-start
  15.1 107.0 %all-gather.3.cloned.1.call-done = f32[128,160,256]{2,1,0:T(8,128)} async-done(((f32[8,160,256]{2,1,0:T(8,128)}), f32[128,160,256]{2,1,0:T(8,128)}) %all-gather.3.cloned.1.call-update) | async-done | bytes 20971536 | tf_op jit(solution)/shard_map/all_gather | solution.py:20
  122.2 11.1 %gather_fusion = f32[48,160,256]{2,1,0:T(8,128)} fusion(f32[128,160,256]{2,1,0:T(8,128)} %all-gather.3.cloned.1.call-done, s32[1024]{0:T(1024)S(1)} %pad_clamp_fusion), kind=kCustom, calls=%fused_computation.clone | custom fusion | bytes 15728832 | tf_op jit(solution)/shard_map/jit(_take)/gather | solution.py:21
  133.3 7.8 %broadcast_select_fusion.1 = f32[48,160,256]{2,1,0:T(8,128)} fusion(f32[48,160,256]{2,1,0:T(8,128)} %gather_fusion, pred[48]{0:T(512)(128)(4,1)S(1)} %compare_and_fusion), kind=kLoop, calls=%fused_computation.6 | loop fusion | flops 1966080 | bytes 15728688 | tf_op jit(solution)/shard_map/jit(_take)/select_n | solution.py:21
  141.1 6.8 %all-to-all-start.1 = ((f32[48,160,256]{2,1,0:T(8,128)}), f32[48,160,256]{2,1,0:T(8,128)}, u32[]{:S(2)}, u32[]{:S(2)}) async-start(f32[48,160,256]{2,1,0:T(8,128)} %broadcast_select_fusion.1), calls=%async_computation.1 | async-start | bytes 15728640 | tf_op jit(solution)/shard_map/all_to_all | solution.py:22
  148.0 87.3 %all-to-all-done.1 = f32[48,160,256]{2,1,0:T(8,128)} async-done(((f32[48,160,256]{2,1,0:T(8,128)}), f32[48,160,256]{2,1,0:T(8,128)}, u32[]{:S(2)}, u32[]{:S(2)}) %all-to-all-start.1) | async-done | bytes 7864352 | tf_op jit(solution)/shard_map/all_to_all | solution.py:22
  235.2 4.1 copy.44
  239.4 8.4 %fusion.2 = f32[4,320,256]{2,1,0:T(8,128)S(1)} fusion(f32[4,6,320,256]{3,2,1,0:T(8,128)S(1)} %bitcast.55, f32[8,6,256,256]{3,2,1,0:T(8,128)} %param.9, s32[]{:T(128)S(6)} %select_n.26), kind=kOutput, calls=%fused_computation.8 | convolution fusion | flops 3019898880 | bytes 15466500 | tf_op jit(solution)/shard_map/jkcb,jkbe->jce/dot_general | solution.py:44
  249.5 18.7 %all_to_all.66 = f32[4,320,256]{2,0,1:T(4,128)S(1)} all-to-all(f32[4,320,256]{2,0,1:T(4,128)S(1)} %copy.46), channel_id=1, replica_groups=mesh['cells'=2,'genes'=16] {'cells'}, dimensions={1} | all-to-all | bytes 2621440 | tf_op jit(solution)/shard_map/all_to_all | solution.py:45
  268.5 1.2 copy.48
  269.7 108.0 %all-gather.5.cloned.1.call-done = f32[128,160,256]{2,1,0:T(8,128)} async-done(((f32[8,160,256]{2,1,0:T(8,128)}), f32[128,160,256]{2,1,0:T(8,128)}) %all-gather.5.cloned.1.call-update) | async-done | bytes 20971536 | tf_op jit(solution)/shard_map/all_gather | solution.py:20
  377.7 11.1 %gather_fusion.1 = f32[48,160,256]{2,1,0:T(8,128)} fusion(f32[128,160,256]{2,1,0:T(8,128)} %all-gather.5.cloned.1.call-done, s32[1024]{0:T(1024)S(1)} %pad_clamp_fusion), kind=kCustom, calls=%fused_computation.1.clone | custom fusion | bytes 15728832 | tf_op jit(solution)/shard_map/jit(_take)/gather | solution.py:21
  388.8 7.8 %broadcast_select_fusion = f32[48,160,256]{2,1,0:T(8,128)} fusion(f32[48,160,256]{2,1,0:T(8,128)} %gather_fusion.1, pred[48]{0:T(512)(128)(4,1)S(1)} %compare_and_fusion), kind=kLoop, calls=%fused_computation.5 | loop fusion | flops 1966080 | bytes 15728688 | tf_op jit(solution)/shard_map/jit(_take)/select_n | solution.py:21
  396.7 6.9 %all-to-all-start.3 = ((f32[48,160,256]{2,1,0:T(8,128)}), f32[48,160,256]{2,1,0:T(8,128)}, u32[]{:S(2)}, u32[]{:S(2)}) async-start(f32[48,160,256]{2,1,0:T(8,128)} %broadcast_select_fusion), calls=%async_computation.3 | async-start | bytes 15728640 | tf_op jit(solution)/shard_map/all_to_all | solution.py:22
  403.7 1.4 multiply_reduce_fusion
  405.1 2.5 fusion.19
  407.6 2.5 copy.45
  410.2 3.3 fusion.9
  413.4 11.5 %fusion.6 = f32[4,6,256,256]{3,2,1,0:T(8,128)} fusion(f32[4,6,320,256]{3,2,1,0:T(8,128)} %bitcast.56, f32[4,320,256]{2,1,0:T(8,128)S(1)} %fusion.5), kind=kOutput, calls=%fused_computation.11 | convolution fusion | flops 3019898880 | bytes 15466496 | tf_op jit(solution)/shard_map/jkcb,jce->jkbe/dot_general | solution.py:49
  425.0 65.9 %all-to-all-done.3 = f32[48,160,256]{2,1,0:T(8,128)} async-done(((f32[48,160,256]{2,1,0:T(8,128)}), f32[48,160,256]{2,1,0:T(8,128)}, u32[]{:S(2)}, u32[]{:S(2)}) %all-to-all-start.3) | async-done | bytes 7864352 | tf_op jit(solution)/shard_map/all_to_all | solution.py:22
  490.8 3.9 copy.49
  495.9 12.7 %clamp_subtract_fusion = f32[4,6,256,256]{3,2,1,0:T(8,128)} fusion(f32[4,6,256,256]{3,2,1,0:T(8,128)S(1)} %copy-done.1, f32[8,6,256,256]{3,2,1,0:T(8,128)} %param.9, s32[]{:T(128)S(6)} %select_n.26, f32[4,6,320,256]{3,2,1,0:T(8,128)S(1)} %bitcast.57, f32[4,320,256,1]{2,1,3,0:T(8,128)S(1)} %bitcast.60), kind=kOutput, calls=%fused_computation.2 | convolution fusion | flops 3027763200 | bytes 28049412 | tf_op jit(solution)/shard_map/jkcb,jce->jkbe/dot_general | solution.py:50
  (32 shorter events, 3.5 us)
Async XLA Ops:
  7.2 7.6 %copy-start.3 = (s32[128,6]{0,1:T(8,128)S(1)}, s32[128,6]{0,1:T(8,128)}, u32[]{:S(2)}) copy-start(s32[128,6]{0,1:T(8,128)} %param.11) | copy-start | bytes 9220
  7.2 7.6 %copy-start.4 = (s32[128,6]{0,1:T(8,128)S(1)}, s32[128,6]{0,1:T(8,128)}, u32[]{:S(2)}) copy-start(s32[128,6]{0,1:T(8,128)} %param.10) | copy-start | bytes 9220
  7.2 115.0 %all-gather.3.cloned.1.call-start = ((), (), s32[]{:S(2)}) async-start(), calls=%async_computation.4 | async-start | bytes 22282240 | tf_op jit(solution)/shard_map/all_gather | solution.py:20
  10.5 130.6 %all-to-all-start = ((f32[8,160,256]{2,1,0:T(8,128)}), f32[8,160,256]{2,1,0:T(8,128)S(1)}, u32[]{:S(2)}, u32[]{:S(2)}) async-start(f32[8,160,256]{2,1,0:T(8,128)} %copy.40), calls=%async_computation | async-start | bytes 2621440 | tf_op jit(solution)/shard_map/all_to_all | solution.py:41
  141.1 94.2 %all-to-all-start.1 = ((f32[48,160,256]{2,1,0:T(8,128)}), f32[48,160,256]{2,1,0:T(8,128)}, u32[]{:S(2)}, u32[]{:S(2)}) async-start(f32[48,160,256]{2,1,0:T(8,128)} %broadcast_select_fusion.1), calls=%async_computation.1 | async-start | bytes 15728640 | tf_op jit(solution)/shard_map/all_to_all | solution.py:22
  147.8 229.9 %all-gather.5.cloned.1.call-start = ((), (), s32[]{:S(2)}) async-start(), calls=%async_computation.5 | async-start | bytes 22282240 | tf_op jit(solution)/shard_map/all_gather | solution.py:20
  239.4 8.5 %copy-start = (f32[24,2,160,256]{3,2,1,0:T(8,128)}, f32[24,2,160,256]{3,2,1,0:T(8,128)S(1)}, u32[]{:S(2)}) copy-start(f32[24,2,160,256]{3,2,1,0:T(8,128)S(1)} %copy.44) | copy-start | bytes 23592964
  239.4 8.5 %copy-start.2 = (f32[8,256,256]{2,1,0:T(8,128)S(1)}, f32[8,256,256]{2,1,0:T(8,128)}, u32[]{:S(2)}) copy-start(f32[8,256,256]{2,1,0:T(8,128)} %param.8) | copy-start | bytes 6291460
  396.7 94.2 %all-to-all-start.3 = ((f32[48,160,256]{2,1,0:T(8,128)}), f32[48,160,256]{2,1,0:T(8,128)}, u32[]{:S(2)}, u32[]{:S(2)}) async-start(f32[48,160,256]{2,1,0:T(8,128)} %broadcast_select_fusion), calls=%async_computation.3 | async-start | bytes 15728640 | tf_op jit(solution)/shard_map/all_to_all | solution.py:22
  490.8 5.0 copy-start.1
Sparse Core Ops, SparseCore 0:
  10.6 111.4 all-gather.2
  269.8 107.8 all-gather.4

commit v2 on v1

--- a/solution.py
+++ b/solution.py
@@ -1,7 +1,13 @@
+import functools
+
 import jax
 import jax.numpy as jnp
 from jax import lax
+from jax.experimental import pallas as pl
+from jax.experimental.pallas import tpu as pltpu
 from jax.sharding import PartitionSpec as P
+
+MESH = pl.DeviceIdType.MESH
 
 
 def stored_rows(omega_src, omega_off, per_dev):
@@ -16,10 +22,204 @@
     return values - jnp.clip(values, -limit, limit)
 
 
-def exchange(shard, table):
-    whole = lax.all_gather(shard, "genes", axis=0, tiled=True)
-    picked = jnp.take(whole, table, axis=0)
-    return lax.all_to_all(picked, "cells", split_axis=0, concat_axis=1, tiled=True)
+def exchange_kernel(chunks, table_ref, shard_ref, far_ref, *scratch):
+    held, picked = scratch[:chunks], scratch[chunks : 2 * chunks]
+    z_send, x_send, k_send, got, c_send, c_got, own_sem = scratch[2 * chunks :]
+    groups, cells = lax.axis_size("genes"), lax.axis_size("cells")
+    me, part = lax.axis_index("genes"), lax.axis_index("cells")
+    line = groups // 4
+    per_dev, cell_rows, _ = shard_ref.shape
+    size = cell_rows // chunks
+    entries = far_ref.shape[0]
+    z, lane = me // 4, me % 4
+    other_x = lane + 2 - 4 * (lane // 2)
+    other_k = me + 1 - 2 * (me % 2)
+    x_peer = z * 4 + other_x
+
+    def to_gene(gene):
+        return (part, gene)
+
+    def to_cell(step):
+        return ((part + step) % cells, me)
+
+    barrier = pltpu.get_barrier_semaphore()
+    ahead, behind = (z + 1) % line * 4 + lane, (z + line - 1) % line * 4 + lane
+    for gene in (ahead, behind, x_peer, other_k):
+        pl.semaphore_signal(barrier, inc=1, device_id=to_gene(gene), device_id_type=MESH)
+    for step in range(1, cells):
+        pl.semaphore_signal(barrier, inc=1, device_id=to_cell(step), device_id_type=MESH)
+    pl.semaphore_wait(barrier, 4 + cells - 1)
+
+    def seat(chunk, gene):
+        return held[chunk].at[pl.ds(gene * per_dev, per_dev)]
+
+    def own(chunk):
+        return shard_ref.at[:, pl.ds(chunk * size, size), :]
+
+    def copy(chunk, gene, send_sem, target, first=False):
+        return pltpu.make_async_remote_copy(
+            src_ref=own(chunk) if first else seat(chunk, gene),
+            dst_ref=seat(chunk, gene),
+            send_sem=send_sem,
+            recv_sem=got.at[chunk, gene],
+            device_id=to_gene(target),
+            device_id_type=MESH,
+        )
+
+    def arrive(chunk, gene):
+        copy(chunk, gene, k_send.at[chunk, gene], other_k).wait_recv()
+
+    def keep(chunk):
+        return pltpu.make_async_copy(own(chunk), seat(chunk, me), own_sem.at[chunk])
+
+    def up(chunk, gene, first=False):
+        return copy(chunk, gene, z_send.at[chunk, gene, 0], me + 4, first)
+
+    def down(chunk, gene, first=False):
+        return copy(chunk, gene, z_send.at[chunk, gene, 1], me - 4, first)
+
+    def across(chunk, gene, first=False):
+        return copy(chunk, gene, x_send.at[chunk, gene], x_peer, first)
+
+    def beside(chunk, gene, first=False):
+        return copy(chunk, gene, k_send.at[chunk, gene], other_k, first)
+
+    def start_own(chunk):
+        pl.when(z < line - 1)(lambda: up(chunk, me, True).start())
+        pl.when(z > 0)(lambda: down(chunk, me, True).start())
+        across(chunk, me, True).start()
+        beside(chunk, me, True).start()
+        keep(chunk).start()
+
+    def relay(chunk, distance):
+        @pl.when(z - distance >= 0)
+        def _():
+            gene = me - 4 * distance
+            arrive(chunk, gene)
+            pl.when(z < line - 1)(lambda: up(chunk, gene).start())
+            across(chunk, gene).start()
+            beside(chunk, gene).start()
+
+        @pl.when(z + distance < line)
+        def _():
+            gene = me + 4 * distance
+            arrive(chunk, gene)
+            pl.when(z > 0)(lambda: down(chunk, gene).start())
+            across(chunk, gene).start()
+            beside(chunk, gene).start()
+
+    def cross_over(chunk):
+        for at in range(line):
+            gene = at * 4 + other_x
+            arrive(chunk, gene)
+            beside(chunk, gene).start()
+
+    def row_span(chunk, cell):
+        return pl.ds(pl.multiple_of(cell * cell_rows + chunk * size, 8), size)
+
+    def hand(chunk, step):
+        return pltpu.make_async_remote_copy(
+            src_ref=picked[chunk].at[step - 1],
+            dst_ref=far_ref.at[:, row_span(chunk, part), :],
+            send_sem=c_send.at[chunk, step],
+            recv_sem=c_got.at[chunk, step],
+            device_id=to_cell(step),
+            device_id_type=MESH,
+        )
+
+    def pick(chunk):
+        keep(chunk).wait()
+        for at in range(line):
+            for side in range(2):
+                arrive(chunk, at * 4 + side * 2 + other_k % 2)
+        for step in list(range(1, cells)) + [0]:
+            base = (part + step) % cells * entries
+
+            def body(entry, carry):
+                block = held[chunk][table_ref[base + entry]]
+                if step == 0:
+                    far_ref[entry, row_span(chunk, part), :] = block
+                else:
+                    picked[chunk][step - 1, entry] = block
+                return carry
+
+            lax.fori_loop(0, entries, body, 0)
+            if step:
+                hand(chunk, step).start()
+
+    for t in range(chunks + line + 1):
+        if t < chunks:
+            start_own(t)
+        for distance in range(1, line):
+            if 0 <= t - distance < chunks:
+                relay(t - distance, distance)
+        if 0 <= t - line < chunks:
+            cross_over(t - line)
+        if 0 <= t - line - 1 < chunks:
+            pick(t - line - 1)
+
+    for chunk in range(chunks):
+        for step in range(1, cells):
+            hand(chunk, step).wait_recv()
+            hand(chunk, step).wait_send()
+        pl.when(z < line - 1)(lambda: up(chunk, me, True).wait_send())
+        pl.when(z > 0)(lambda: down(chunk, me, True).wait_send())
+        across(chunk, me, True).wait_send()
+        beside(chunk, me, True).wait_send()
+        for distance in range(1, line):
+
+            @pl.when(z - distance >= 0)
+            def _():
+                gene = me - 4 * distance
+                pl.when(z < line - 1)(lambda: up(chunk, gene).wait_send())
+                across(chunk, gene).wait_send()
+                beside(chunk, gene).wait_send()
+
+            @pl.when(z + distance < line)
+            def _():
+                gene = me + 4 * distance
+                pl.when(z > 0)(lambda: down(chunk, gene).wait_send())
+                across(chunk, gene).wait_send()
+                beside(chunk, gene).wait_send()
+
+        for at in range(line):
+            beside(chunk, at * 4 + other_x).wait_send()
+
+
+def exchange(shard, table, which):
+    groups, cells = lax.axis_size("genes"), lax.axis_size("cells")
+    per_dev, cell_rows, width = shard.shape
+    entries = table.shape[0] // cells
+    if groups % 4 or groups < 8 or cell_rows % 8:
+        whole = lax.all_gather(shard, "genes", axis=0, tiled=True)
+        picked = jnp.take(whole, table, axis=0)
+        return lax.all_to_all(picked, "cells", split_axis=0, concat_axis=1, tiled=True)
+    chunks = max(c for c in range(1, 6) if cell_rows % (8 * c) == 0)
+    size = cell_rows // chunks
+    dma = pltpu.SemaphoreType.DMA
+    return pl.pallas_call(
+        functools.partial(exchange_kernel, chunks),
+        out_shape=jax.ShapeDtypeStruct((entries, cells * cell_rows, width), shard.dtype),
+        in_specs=[
+            pl.BlockSpec(memory_space=pltpu.SMEM),
+            pl.BlockSpec(memory_space=pltpu.VMEM),
+        ],
+        out_specs=pl.BlockSpec(memory_space=pltpu.VMEM),
+        scratch_shapes=[pltpu.VMEM((groups * per_dev, size, width), shard.dtype)] * chunks
+        + [pltpu.VMEM((cells - 1, entries, size, width), shard.dtype)] * chunks
+        + [
+            dma((chunks, groups, 2)),
+            dma((chunks, groups)),
+            dma((chunks, groups)),
+            dma((chunks, groups)),
+            dma((chunks, cells)),
+            dma((chunks, cells)),
+            dma((chunks,)),
+        ],
+        compiler_params=pltpu.CompilerParams(
+            collective_id=which, has_side_effects=True, vmem_limit_bytes=60 << 20
+        ),
+    )(table, shard)
 
 
 def per_device(expression, omega_diag, omega_offd, omega_src, omega_off):
@@ -39,11 +239,11 @@
 
     shard_x = jnp.swapaxes(expression.reshape(cell_rows, per_dev, width), 0, 1)
     own_x = lax.all_to_all(shard_x, "cells", split_axis=0, concat_axis=1, tiled=True)
-    far_x = exchange(shard_x, table).reshape(share, fan, all_rows, width)
+    far_x = exchange(shard_x, table, 0).reshape(share, fan, all_rows, width)
     own_y = jnp.einsum("jcb,jbe->jce", own_x, mine_diag, precision=high)
     own_y = own_y + jnp.einsum("jkcb,jkbe->jce", far_x, mine_off, precision=high)
     shard_y = lax.all_to_all(own_y, "cells", split_axis=1, concat_axis=0, tiled=True)
-    far_y = exchange(shard_y, table).reshape(share, fan, all_rows, width)
+    far_y = exchange(shard_y, table, 1).reshape(share, fan, all_rows, width)
     diag_sum = jnp.einsum("jcb,jce->jbe", own_x, own_y, precision=high)
     diag_sum = diag_sum + jnp.swapaxes(diag_sum, 1, 2)
     off_sum = jnp.einsum("jkcb,jce->jkbe", far_x, own_y, precision=high)

time: 516 us -> 420 us (0.81)
  waiting for transfers between devices: 368 us -> 0.01 us
  Pallas kernels: 0 us -> 353 us
  local copies, waits for them, and re-layouts: 39.8 us -> 11.7 us
  blocking collectives: 18.7 us -> 0 us
  other arithmetic: 20.4 us -> 4.77 us
  between operations: 14.2 us -> 0.73 us
  starting transfers between devices: 18.1 us -> 9.13 us
    pallas_call x0 -> x2, Pallas kernels: none -> 353 us  [exchange(): pl.pallas_call(functools.partial(exchange_kernel, chunks), out_shape=jax....]
    all_gather x2 -> x0, waiting for transfers between devices: 215 us -> none  [exchange(): whole = lax.all_gather(shard, 'genes', axis=0, tiled=True)]
    all_to_all x2 -> x1, waiting for transfers between devices: 153 us -> 0.01 us  [per_device(): lax.all_to_all(own_y, 'cells', split_axis=1, concat_axis=0, tiled=True)]
    gather x2 -> x0, local copies, waits for them, and re-layouts: 22.2 us -> none  [exchange(): picked = jnp.take(whole, table, axis=0)]
    all_to_all x1 -> x0, blocking collectives: 18.7 us -> none  [per_device(): lax.all_to_all(own_y, 'cells', split_axis=1, concat_axis=0, tiled=True)]
    select_n x3 -> x0, other arithmetic: 15.6 us -> none  [exchange(): picked = jnp.take(whole, table, axis=0)]
    all_to_all x2 -> x1, starting transfers between devices: 13.7 us -> 4.74 us  [per_device(): lax.all_to_all(own_y, 'cells', split_axis=1, concat_axis=0, tiled=True)]
    all_to_all x2 -> x0, local copies, waits for them, and re-layouts: 8.05 us -> none  [exchange(): lax.all_to_all(picked, 'cells', split_axis=0, concat_axis=1, tiled=True)]
  transfers between devices with their start and end apart: 5 -> 2, of which waited for: 4 -> 0; matrix products, arithmetic and copies ran while one was open for 8% -> 7% of each run, Pallas kernels for 0% -> 43%
where the time goes in v2:
time: 420 us
  Pallas kernels  353 us (84%)
  matrix products  40 us (10%)
  local copies, waits for them, and re-layouts  11.7 us (3%)
  starting transfers between devices  9.13 us (2%)
  other arithmetic  4.77 us (1%)
    pallas_call x2, Pallas kernels, exchange(): pl.pallas_call(functools.partial(exchange_kernel, chunks), out_shape=jax....  353 us
    dot_general x1, matrix products, per_device(): jnp.einsum('jkcb,jce->jkbe', far_y, own_x, precision=high)  14.1 us
    dot_general x1, matrix products, per_device(): off_sum = jnp.einsum('jkcb,jce->jkbe', far_x, own_y, precision=high)  11.5 us
    dot_general x1, matrix products, per_device(): jnp.einsum('jkcb,jkbe->jce', far_x, mine_off, precision=high)  9.85 us
  transfers between devices with their start and end apart: 2, of which 0 were waited for; matrix products, arithmetic and copies ran while one was open for 7% of the time, Pallas kernels for 43%

profile of v2, /device:TPU:0, one launch (start us, length us, event | category | flops | bytes accessed | tf_op | source)
XLA Modules:
  0.0 419.7 jit_solution(494636611043356090)
XLA Ops:
  0.6 2.5 copy.27
  3.1 4.4 %all-to-all-start = ((f32[8,160,256]{2,1,0:T(8,128)}), f32[8,160,256]{2,1,0:T(8,128)S(1)}, u32[]{:S(2)}, u32[]{:S(2)}) async-start(f32[8,160,256]{2,1,0:T(8,128)} %bitcast.51.shard_ref), calls=%async_computation | async-start | bytes 2621440 | tf_op jit(solution)/shard_map/all_to_all | solution.py:241
  7.6 1.4 multiply_reduce_fusion
  9.0 0.0 copy-done.1
  9.0 0.0 copy-done.2
  9.1 0.1 constant_dynamic-slice_fusion
  9.1 0.1 copy.18
  9.2 0.7 reshape.33.table_ref
  9.9 179.0 %shard_map.68 = f32[24,320,256]{2,1,0:T(8,128)} custom-call(s32[48]{0:T(128)} %reshape.33.table_ref, f32[8,160,256]{2,1,0:T(8,128)} %bitcast.51.shard_ref), custom_call_target="tpu_custom_call" | custom-call | tf_op jit(solution)/shard_map/pallas_call | solution.py:200
  188.9 9.9 %fusion.2 = f32[4,320,256]{2,1,0:T(8,128)} fusion(f32[4,6,320,256]{3,2,1,0:T(8,128)} %bitcast.52, f32[8,6,256,256]{3,2,1,0:T(8,128)} %param.7, s32[]{:T(128)S(6)} %select_n.19), kind=kOutput, calls=%fused_computation.4 | convolution fusion | flops 3019898880 | bytes 15466500 | tf_op jit(solution)/shard_map/jkcb,jkbe->jce/dot_general | solution.py:244
  198.8 0.0 all-to-all-done
  198.8 0.1 copy.17
  198.9 1.2 copy-done
  200.1 2.0 fusion.5
  202.1 2.5 fusion.19
  204.6 1.9 copy.20
  206.5 4.7 %all-to-all-start.1 = ((f32[4,320,256]{2,0,1:T(4,128)}), f32[4,320,256]{2,0,1:T(4,128)}, u32[]{:S(2)}, u32[]{:S(2)}) async-start(f32[4,320,256]{2,0,1:T(4,128)} %copy.20), calls=%async_computation.1 | async-start | bytes 2621440 | tf_op jit(solution)/shard_map/all_to_all | solution.py:245
  211.2 2.5 copy.19
  213.8 3.3 fusion.9
  217.0 11.5 %fusion.6 = f32[4,6,256,256]{3,2,1,0:T(8,128)} fusion(f32[4,6,320,256]{3,2,1,0:T(8,128)} %bitcast.53, f32[4,320,256]{2,1,0:T(8,128)S(1)} %fusion.5), kind=kOutput, calls=%fused_computation.8 | convolution fusion | flops 3019898880 | bytes 15466496 | tf_op jit(solution)/shard_map/jkcb,jce->jkbe/dot_general | solution.py:249
  228.6 0.0 all-to-all-done.1
  228.6 2.6 copy.21
  231.2 174.4 %shard_map.69 = f32[24,320,256]{2,1,0:T(8,128)} custom-call(s32[48]{0:T(128)} %reshape.33.table_ref, f32[8,160,256]{2,1,0:T(8,128)} %bitcast.58), custom_call_target="tpu_custom_call" | custom-call | tf_op jit(solution)/shard_map/pallas_call | solution.py:200
  405.6 14.1 %clamp_subtract_fusion = f32[4,6,256,256]{3,2,1,0:T(8,128)} fusion(f32[4,6,256,256]{3,2,1,0:T(8,128)} %fusion.6, f32[8,6,256,256]{3,2,1,0:T(8,128)} %param.7, s32[]{:T(128)S(6)} %select_n.19, f32[4,6,320,256]{3,2,1,0:T(8,128)} %bitcast.54, f32[4,320,256,1]{2,1,3,0:T(8,128)S(1)} %bitcast.57), kind=kOutput, calls=%fused_computation | convolution fusion | flops 3027763200 | bytes 28049412 | tf_op jit(solution)/shard_map/jkcb,jce->jkbe/dot_general | solution.py:250
  (10 shorter events, 0.1 us)
Async XLA Ops:
  3.1 5.9 %copy-start.1 = (s32[128,6]{0,1:T(8,128)S(1)}, s32[128,6]{0,1:T(8,128)}, u32[]{:S(2)}) copy-start(s32[128,6]{0,1:T(8,128)} %param.9) | copy-start | bytes 9220
  3.1 5.9 %copy-start.2 = (s32[128,6]{0,1:T(8,128)S(1)}, s32[128,6]{0,1:T(8,128)}, u32[]{:S(2)}) copy-start(s32[128,6]{0,1:T(8,128)} %param.8) | copy-start | bytes 9220
  3.1 195.7 %all-to-all-start = ((f32[8,160,256]{2,1,0:T(8,128)}), f32[8,160,256]{2,1,0:T(8,128)S(1)}, u32[]{:S(2)}, u32[]{:S(2)}) async-start(f32[8,160,256]{2,1,0:T(8,128)} %bitcast.51.shard_ref), calls=%async_computation | async-start | bytes 2621440 | tf_op jit(solution)/shard_map/all_to_all | solution.py:241
  198.8 1.3 copy-start
  206.5 22.1 %all-to-all-start.1 = ((f32[4,320,256]{2,0,1:T(4,128)}), f32[4,320,256]{2,0,1:T(4,128)}, u32[]{:S(2)}, u32[]{:S(2)}) async-start(f32[4,320,256]{2,0,1:T(4,128)} %copy.20), calls=%async_computation.1 | async-start | bytes 2621440 | tf_op jit(solution)/shard_map/all_to_all | solution.py:245

commit v3 on v2

--- a/solution.py
+++ b/solution.py
@@ -91,28 +91,35 @@
         beside(chunk, me, True).start()
         keep(chunk).start()
 
-    def relay(chunk, distance):
-        @pl.when(z - distance >= 0)
-        def _():
-            gene = me - 4 * distance
-            arrive(chunk, gene)
-            pl.when(z < line - 1)(lambda: up(chunk, gene).start())
-            across(chunk, gene).start()
-            beside(chunk, gene).start()
-
-        @pl.when(z + distance < line)
-        def _():
-            gene = me + 4 * distance
-            arrive(chunk, gene)
-            pl.when(z > 0)(lambda: down(chunk, gene).start())
-            across(chunk, gene).start()
-            beside(chunk, gene).start()
-
-    def cross_over(chunk):
-        for at in range(line):
-            gene = at * 4 + other_x
-            arrive(chunk, gene)
-            beside(chunk, gene).start()
+    def turned(chunk):
+        return chunk % 5 == 3
+
+    def lanes(chunk):
+        return (0, other_x - lane) if turned(chunk) else (0,)
+
+    def line_hops(chunk, distance, act):
+        def hops(gene, edge, onward):
+            for shift in lanes(chunk):
+                act[0](chunk, gene + shift)
+                pl.when(edge)(lambda: act[1](onward(chunk, gene + shift)))
+                if not turned(chunk):
+                    act[1](across(chunk, gene))
+                act[1](beside(chunk, gene + shift))
+
+        pl.when(z - distance >= 0)(lambda: hops(me - 4 * distance, z < line - 1, up))
+        pl.when(z + distance < line)(lambda: hops(me + 4 * distance, z > 0, down))
+
+    def cross_hops(chunk, act):
+        for at in range(1 if turned(chunk) else line):
+            gene = x_peer if turned(chunk) else at * 4 + other_x
+            act[0](chunk, gene)
+            if turned(chunk):
+                pl.when(z < line - 1)(lambda: act[1](up(chunk, gene)))
+                pl.when(z > 0)(lambda: act[1](down(chunk, gene)))
+            act[1](beside(chunk, gene))
+
+    start = (arrive, lambda c: c.start())
+    finish = (lambda chunk, gene: None, lambda c: c.wait_send())
 
     def row_span(chunk, cell):
         return pl.ds(pl.multiple_of(cell * cell_rows + chunk * size, 8), size)
@@ -150,11 +157,14 @@
     for t in range(chunks + line + 1):
         if t < chunks:
             start_own(t)
+        if t >= 1 and t - 1 < chunks and turned(t - 1):
+            cross_hops(t - 1, start)
         for distance in range(1, line):
-            if 0 <= t - distance < chunks:
-                relay(t - distance, distance)
-        if 0 <= t - line < chunks:
-            cross_over(t - line)
+            chunk = t - distance
+            if 0 <= chunk < chunks:
+                line_hops(chunk, distance, start)
+        if 0 <= t - line < chunks and not turned(t - line):
+            cross_hops(t - line, start)
         if 0 <= t - line - 1 < chunks:
             pick(t - line - 1)
 
@@ -167,23 +177,8 @@
         across(chunk, me, True).wait_send()
         beside(chunk, me, True).wait_send()
         for distance in range(1, line):
-
-            @pl.when(z - distance >= 0)
-            def _():
-                gene = me - 4 * distance
-                pl.when(z < line - 1)(lambda: up(chunk, gene).wait_send())
-                across(chunk, gene).wait_send()
-                beside(chunk, gene).wait_send()
-
-            @pl.when(z + distance < line)
-            def _():
-                gene = me + 4 * distance
-                pl.when(z > 0)(lambda: down(chunk, gene).wait_send())
-                across(chunk, gene).wait_send()
-                beside(chunk, gene).wait_send()
-
-        for at in range(line):
-            beside(chunk, at * 4 + other_x).wait_send()
+            line_hops(chunk, distance, finish)
+        cross_hops(chunk, finish)
 
 
 def exchange(shard, table, which):
@@ -194,7 +189,7 @@
         whole = lax.all_gather(shard, "genes", axis=0, tiled=True)
         picked = jnp.take(whole, table, axis=0)
         return lax.all_to_all(picked, "cells", split_axis=0, concat_axis=1, tiled=True)
-    chunks = max(c for c in range(1, 6) if cell_rows % (8 * c) == 0)
+    chunks = max(c for c in range(1, 11) if cell_rows % (8 * c) == 0)
     size = cell_rows // chunks
     dma = pltpu.SemaphoreType.DMA
     return pl.pallas_call(

time: 420 us -> 366 us (0.87)
  Pallas kernels: 353 us -> 299 us
    pallas_call x2, Pallas kernels: 353 us -> 299 us  [exchange(): pl.pallas_call(functools.partial(exchange_kernel, chunks), out_shape=jax....]
  transfers between devices with their start and end apart: 2 -> 2, of which waited for: 0 -> 0; matrix products, arithmetic and copies ran while one was open for 7% -> 8% of each run, Pallas kernels for 43% -> 41%
where the time goes in v3:
time: 366 us; the launch traced here: 365 us
  Pallas kernels  299 us (82%)
  matrix products  40.2 us (11%)
  local copies, waits for them, and re-layouts  11.7 us (3%)
  starting transfers between devices  9.13 us (2%)
  other arithmetic  4.77 us (1%)
    pallas_call x2, Pallas kernels, exchange(): pl.pallas_call(functools.partial(exchange_kernel, chunks), out_shape=jax....  299 us
    dot_general x1, matrix products, per_device(): jnp.einsum('jkcb,jce->jkbe', far_y, own_x, precision=high)  14.4 us
    dot_general x1, matrix products, per_device(): off_sum = jnp.einsum('jkcb,jce->jkbe', far_x, own_y, precision=high)  11.5 us
    dot_general x1, matrix products, per_device(): jnp.einsum('jkcb,jkbe->jce', far_x, mine_off, precision=high)  9.85 us
  transfers between devices with their start and end apart: 2, of which 0 were waited for; matrix products, arithmetic and copies ran while one was open for 8% of the time, Pallas kernels for 41%

profile of v3, /device:TPU:0, one launch (start us, length us, event | category | flops | bytes accessed | tf_op | source)
XLA Modules:
  0.0 365.2 jit_solution(949663662592855235)
XLA Ops:
  0.6 2.5 copy.27
  3.1 4.4 %all-to-all-start = ((f32[8,160,256]{2,1,0:T(8,128)}), f32[8,160,256]{2,1,0:T(8,128)S(1)}, u32[]{:S(2)}, u32[]{:S(2)}) async-start(f32[8,160,256]{2,1,0:T(8,128)} %bitcast.51.shard_ref), calls=%async_computation | async-start | bytes 2621440 | tf_op jit(solution)/shard_map/all_to_all | solution.py:236
  7.6 1.4 multiply_reduce_fusion
  9.0 0.0 copy-done.1
  9.0 0.0 copy-done.2
  9.1 0.1 constant_dynamic-slice_fusion
  9.1 0.1 copy.18
  9.2 0.7 reshape.33.table_ref
  9.9 150.6 %shard_map.68 = f32[24,320,256]{2,1,0:T(8,128)} custom-call(s32[48]{0:T(128)} %reshape.33.table_ref, f32[8,160,256]{2,1,0:T(8,128)} %bitcast.51.shard_ref), custom_call_target="tpu_custom_call" | custom-call | tf_op jit(solution)/shard_map/pallas_call | solution.py:195
  160.6 9.9 %fusion.2 = f32[4,320,256]{2,1,0:T(8,128)} fusion(f32[4,6,320,256]{3,2,1,0:T(8,128)} %bitcast.52, f32[8,6,256,256]{3,2,1,0:T(8,128)} %param.7, s32[]{:T(128)S(6)} %select_n.19), kind=kOutput, calls=%fused_computation.4 | convolution fusion | flops 3019898880 | bytes 15466500 | tf_op jit(solution)/shard_map/jkcb,jkbe->jce/dot_general | solution.py:239
  170.4 0.0 all-to-all-done
  170.4 0.1 copy.17
  170.5 1.2 copy-done
  171.7 2.0 fusion.5
  173.7 2.5 fusion.19
  176.2 1.9 copy.20
  178.1 4.7 %all-to-all-start.1 = ((f32[4,320,256]{2,0,1:T(4,128)}), f32[4,320,256]{2,0,1:T(4,128)}, u32[]{:S(2)}, u32[]{:S(2)}) async-start(f32[4,320,256]{2,0,1:T(4,128)} %copy.20), calls=%async_computation.1 | async-start | bytes 2621440 | tf_op jit(solution)/shard_map/all_to_all | solution.py:240
  182.9 2.5 copy.19
  185.4 3.3 fusion.9
  188.7 11.5 %fusion.6 = f32[4,6,256,256]{3,2,1,0:T(8,128)} fusion(f32[4,6,320,256]{3,2,1,0:T(8,128)} %bitcast.53, f32[4,320,256]{2,1,0:T(8,128)S(1)} %fusion.5), kind=kOutput, calls=%fused_computation.8 | convolution fusion | flops 3019898880 | bytes 15466496 | tf_op jit(solution)/shard_map/jkcb,jce->jkbe/dot_general | solution.py:244
  200.2 0.0 all-to-all-done.1
  200.2 2.6 copy.21
  202.8 148.0 %shard_map.69 = f32[24,320,256]{2,1,0:T(8,128)} custom-call(s32[48]{0:T(128)} %reshape.33.table_ref, f32[8,160,256]{2,1,0:T(8,128)} %bitcast.58), custom_call_target="tpu_custom_call" | custom-call | tf_op jit(solution)/shard_map/pallas_call | solution.py:195
  350.9 14.4 %clamp_subtract_fusion = f32[4,6,256,256]{3,2,1,0:T(8,128)} fusion(f32[4,6,256,256]{3,2,1,0:T(8,128)} %fusion.6, f32[8,6,256,256]{3,2,1,0:T(8,128)} %param.7, s32[]{:T(128)S(6)} %select_n.19, f32[4,6,320,256]{3,2,1,0:T(8,128)} %bitcast.54, f32[4,320,256,1]{2,1,3,0:T(8,128)S(1)} %bitcast.57), kind=kOutput, calls=%fused_computation | convolution fusion | flops 3027763200 | bytes 28049412 | tf_op jit(solution)/shard_map/jkcb,jce->jkbe/dot_general | solution.py:245
  (10 shorter events, 0.1 us)
Async XLA Ops:
  3.1 5.9 %copy-start.1 = (s32[128,6]{0,1:T(8,128)S(1)}, s32[128,6]{0,1:T(8,128)}, u32[]{:S(2)}) copy-start(s32[128,6]{0,1:T(8,128)} %param.9) | copy-start | bytes 9220
  3.1 5.9 %copy-start.2 = (s32[128,6]{0,1:T(8,128)S(1)}, s32[128,6]{0,1:T(8,128)}, u32[]{:S(2)}) copy-start(s32[128,6]{0,1:T(8,128)} %param.8) | copy-start | bytes 9220
  3.1 167.3 %all-to-all-start = ((f32[8,160,256]{2,1,0:T(8,128)}), f32[8,160,256]{2,1,0:T(8,128)S(1)}, u32[]{:S(2)}, u32[]{:S(2)}) async-start(f32[8,160,256]{2,1,0:T(8,128)} %bitcast.51.shard_ref), calls=%async_computation | async-start | bytes 2621440 | tf_op jit(solution)/shard_map/all_to_all | solution.py:236
  170.4 1.3 copy-start
  178.1 22.1 %all-to-all-start.1 = ((f32[4,320,256]{2,0,1:T(4,128)}), f32[4,320,256]{2,0,1:T(4,128)}, u32[]{:S(2)}, u32[]{:S(2)}) async-start(f32[4,320,256]{2,0,1:T(4,128)} %copy.20), calls=%async_computation.1 | async-start | bytes 2621440 | tf_op jit(solution)/shard_map/all_to_all | solution.py:240

commit v4 on v3

--- a/solution.py
+++ b/solution.py
@@ -154,7 +154,7 @@
             if step:
                 hand(chunk, step).start()
 
-    for t in range(chunks + line + 1):
+    for t in range(chunks + line):
         if t < chunks:
             start_own(t)
         if t >= 1 and t - 1 < chunks and turned(t - 1):
@@ -165,8 +165,8 @@
                 line_hops(chunk, distance, start)
         if 0 <= t - line < chunks and not turned(t - line):
             cross_hops(t - line, start)
-        if 0 <= t - line - 1 < chunks:
-            pick(t - line - 1)
+        if 0 <= t - line < chunks:
+            pick(t - line)
 
     for chunk in range(chunks):
         for step in range(1, cells):

time: 366 us -> 355 us (0.970)
  Pallas kernels: 299 us -> 287 us
    pallas_call x2, Pallas kernels: 299 us -> 287 us  [exchange(): pl.pallas_call(functools.partial(exchange_kernel, chunks), out_shape=jax....]
  transfers between devices with their start and end apart: 2 -> 2, of which waited for: 0 -> 1; matrix products, arithmetic and copies ran while one was open for 8% -> 8% of each run, Pallas kernels for 41% -> 41%
where the time goes in v4:
time: 355 us; the launch traced here: 353 us
  Pallas kernels  287 us (81%)
  matrix products  40.2 us (11%)
  local copies, waits for them, and re-layouts  11.7 us (3%)
  starting transfers between devices  9.13 us (3%)
  other arithmetic  4.77 us (1%)
    pallas_call x2, Pallas kernels, exchange(): pl.pallas_call(functools.partial(exchange_kernel, chunks), out_shape=jax....  287 us
    dot_general x1, matrix products, per_device(): jnp.einsum('jkcb,jce->jkbe', far_y, own_x, precision=high)  14.4 us
    dot_general x1, matrix products, per_device(): off_sum = jnp.einsum('jkcb,jce->jkbe', far_x, own_y, precision=high)  11.5 us
    dot_general x1, matrix products, per_device(): jnp.einsum('jkcb,jkbe->jce', far_x, mine_off, precision=high)  9.85 us
  transfers between devices with their start and end apart: 2, of which 1 were waited for; matrix products, arithmetic and copies ran while one was open for 8% of the time, Pallas kernels for 41%

profile of v4, /device:TPU:0, one launch (start us, length us, event | category | flops | bytes accessed | tf_op | source)
XLA Modules:
  0.0 353.4 jit_solution(13630689424054336397)
XLA Ops:
  0.6 2.5 copy.27
  3.1 4.4 %all-to-all-start = ((f32[8,160,256]{2,1,0:T(8,128)}), f32[8,160,256]{2,1,0:T(8,128)S(1)}, u32[]{:S(2)}, u32[]{:S(2)}) async-start(f32[8,160,256]{2,1,0:T(8,128)} %bitcast.51.shard_ref), calls=%async_computation | async-start | bytes 2621440 | tf_op jit(solution)/shard_map/all_to_all | solution.py:236
  7.6 1.4 multiply_reduce_fusion
  9.0 0.0 copy-done.1
  9.0 0.0 copy-done.2
  9.1 0.1 constant_dynamic-slice_fusion
  9.1 0.1 copy.18
  9.2 0.7 reshape.33.table_ref
  9.9 143.5 %shard_map.68 = f32[24,320,256]{2,1,0:T(8,128)} custom-call(s32[48]{0:T(128)} %reshape.33.table_ref, f32[8,160,256]{2,1,0:T(8,128)} %bitcast.51.shard_ref), custom_call_target="tpu_custom_call" | custom-call | tf_op jit(solution)/shard_map/pallas_call | solution.py:195
  153.5 9.9 %fusion.2 = f32[4,320,256]{2,1,0:T(8,128)} fusion(f32[4,6,320,256]{3,2,1,0:T(8,128)} %bitcast.52, f32[8,6,256,256]{3,2,1,0:T(8,128)} %param.7, s32[]{:T(128)S(6)} %select_n.19), kind=kOutput, calls=%fused_computation.4 | convolution fusion | flops 3019898880 | bytes 15466500 | tf_op jit(solution)/shard_map/jkcb,jkbe->jce/dot_general | solution.py:239
  163.3 0.0 all-to-all-done
  163.3 0.1 copy.17
  163.4 1.2 copy-done
  164.6 2.0 fusion.5
  166.6 2.5 fusion.19
  169.1 1.9 copy.20
  171.0 4.7 %all-to-all-start.1 = ((f32[4,320,256]{2,0,1:T(4,128)}), f32[4,320,256]{2,0,1:T(4,128)}, u32[]{:S(2)}, u32[]{:S(2)}) async-start(f32[4,320,256]{2,0,1:T(4,128)} %copy.20), calls=%async_computation.1 | async-start | bytes 2621440 | tf_op jit(solution)/shard_map/all_to_all | solution.py:240
  175.8 2.5 copy.19
  178.3 3.3 fusion.9
  181.5 11.5 %fusion.6 = f32[4,6,256,256]{3,2,1,0:T(8,128)} fusion(f32[4,6,320,256]{3,2,1,0:T(8,128)} %bitcast.53, f32[4,320,256]{2,1,0:T(8,128)S(1)} %fusion.5), kind=kOutput, calls=%fused_computation.8 | convolution fusion | flops 3019898880 | bytes 15466496 | tf_op jit(solution)/shard_map/jkcb,jce->jkbe/dot_general | solution.py:244
  193.1 0.4 all-to-all-done.1
  193.5 2.6 copy.21
  196.1 143.0 %shard_map.69 = f32[24,320,256]{2,1,0:T(8,128)} custom-call(s32[48]{0:T(128)} %reshape.33.table_ref, f32[8,160,256]{2,1,0:T(8,128)} %bitcast.58), custom_call_target="tpu_custom_call" | custom-call | tf_op jit(solution)/shard_map/pallas_call | solution.py:195
  339.1 14.4 %clamp_subtract_fusion = f32[4,6,256,256]{3,2,1,0:T(8,128)} fusion(f32[4,6,256,256]{3,2,1,0:T(8,128)} %fusion.6, f32[8,6,256,256]{3,2,1,0:T(8,128)} %param.7, s32[]{:T(128)S(6)} %select_n.19, f32[4,6,320,256]{3,2,1,0:T(8,128)} %bitcast.54, f32[4,320,256,1]{2,1,3,0:T(8,128)S(1)} %bitcast.57), kind=kOutput, calls=%fused_computation | convolution fusion | flops 3027763200 | bytes 28049412 | tf_op jit(solution)/shard_map/jkcb,jce->jkbe/dot_general | solution.py:245
  (10 shorter events, 0.1 us)
Async XLA Ops:
  3.1 5.9 %copy-start.1 = (s32[128,6]{0,1:T(8,128)S(1)}, s32[128,6]{0,1:T(8,128)}, u32[]{:S(2)}) copy-start(s32[128,6]{0,1:T(8,128)} %param.9) | copy-start | bytes 9220
  3.1 5.9 %copy-start.2 = (s32[128,6]{0,1:T(8,128)S(1)}, s32[128,6]{0,1:T(8,128)}, u32[]{:S(2)}) copy-start(s32[128,6]{0,1:T(8,128)} %param.8) | copy-start | bytes 9220
  3.1 160.2 %all-to-all-start = ((f32[8,160,256]{2,1,0:T(8,128)}), f32[8,160,256]{2,1,0:T(8,128)S(1)}, u32[]{:S(2)}, u32[]{:S(2)}) async-start(f32[8,160,256]{2,1,0:T(8,128)} %bitcast.51.shard_ref), calls=%async_computation | async-start | bytes 2621440 | tf_op jit(solution)/shard_map/all_to_all | solution.py:236
  163.3 1.3 copy-start
  171.0 22.5 %all-to-all-start.1 = ((f32[4,320,256]{2,0,1:T(4,128)}), f32[4,320,256]{2,0,1:T(4,128)}, u32[]{:S(2)}, u32[]{:S(2)}) async-start(f32[4,320,256]{2,0,1:T(4,128)} %copy.20), calls=%async_computation.1 | async-start | bytes 2621440 | tf_op jit(solution)/shard_map/all_to_all | solution.py:240
